TPU v7x, 32 devices: a whole 2x2x4 slice. The times are simulated.
32 devices in a mesh: node: 8 (over z, x), hid: 4 (over y, core).
Axes of the slice: x: 2, y: 2, z: 4, core: 2. Of those that a mesh axis runs over, the one named last changes fastest.
Arguments:
- node_in: bfloat16 [1280, 6, 512], P('node'), may hold values from -6 to 6
- edge_in: bfloat16 [10240, 512], P('node'), may hold values from -6 to 6
- cotangent: bfloat16 [1280, 6, 512], P(('node', 'hid')), may hold values from -6 to 6
- ocean_mask: int32 [1280], P(('node', 'hid')), may hold values 0 or 1
- present_mask: int32 [1280, 6], P(('node', 'hid')), may hold values 0 or 1
- valid_counts: int32 [6], replicated, may hold values from 640 to 1280
- send_slot: int32 [10240], P('node'), may hold values from 0 to 239, as said below
- recv_local: int32 [10240], P('node'), may hold values from 0 to 159, as said below
- halo_lists: int32 [16, 40], P('node'), may hold values from 0 to 159, as said below
- edge_first: float32 [2, 1536, 512], P(None, 'node', 'hid'), may hold values from -0.15625 to 0.15625
- edge_second: float32 [2, 512, 512], P(None, 'hid', 'node'), may hold values from -0.25 to 0.25
- node_first: float32 [2, 1024, 512], P(None, 'node', 'hid'), may hold values from -0.1875 to 0.1875
- node_second: float32 [2, 512, 512], P(None, 'hid', 'node'), may hold values from -0.25 to 0.25
- edge_first_m: float32 [2, 1536, 512], P(None, 'node', 'hid'), may hold values from -512 to 512
- edge_second_m: float32 [2, 512, 512], P(None, 'hid', 'node'), may hold values from -512 to 512
- node_first_m: float32 [2, 1024, 512], P(None, 'node', 'hid'), may hold values from -640 to 640
- node_second_m: float32 [2, 512, 512], P(None, 'hid', 'node'), may hold values from -640 to 640
- edge_first_v: float32 [2, 1536, 512], P(None, 'node', 'hid'), may hold values from 7372.8 to 30720
- edge_second_v: float32 [2, 512, 512], P(None, 'hid', 'node'), may hold values from 7372.8 to 30720
- node_first_v: float32 [2, 1024, 512], P(None, 'node', 'hid'), may hold values from 11059.2 to 44236.8
- node_second_v: float32 [2, 512, 512], P(None, 'hid', 'node'), may hold values from 11059.2 to 44236.8
- small_params: float32 [2, 8, 512], replicated, may hold values from -1.2 to 1.6
- small_m: float32 [2, 8, 512], replicated, may hold values from -448 to 448
- small_v: float32 [2, 8, 512], replicated, may hold values from 614.4 to 24576
- learn_rate: float32 [1], replicated, may hold values from 0.2 to 0.5
Outputs:
- node_out: bfloat16 [1280, 6, 512], P(('node', 'hid'))
- grad_node: bfloat16 [1280, 6, 512], P(('node', 'hid'))
- grad_edge: bfloat16 [10240, 512], P(('node', 'hid'))
- edge_first_new: float32 [2, 1536, 512], P(None, 'node', 'hid')
- edge_second_new: float32 [2, 512, 512], P(None, 'hid', 'node')
- node_first_new: float32 [2, 1024, 512], P(None, 'node', 'hid')
- node_second_new: float32 [2, 512, 512], P(None, 'hid', 'node')
- edge_first_m_new: float32 [2, 1536, 512], P(None, 'node', 'hid')
- edge_second_m_new: float32 [2, 512, 512], P(None, 'hid', 'node')
- node_first_m_new: float32 [2, 1024, 512], P(None, 'node', 'hid')
- node_second_m_new: float32 [2, 512, 512], P(None, 'hid', 'node')
- edge_first_v_new: float32 [2, 1536, 512], P(None, 'node', 'hid')
- edge_second_v_new: float32 [2, 512, 512], P(None, 'hid', 'node')
- node_first_v_new: float32 [2, 1024, 512], P(None, 'node', 'hid')
- node_second_v_new: float32 [2, 512, 512], P(None, 'hid', 'node')
- edge_first_copy: bfloat16 [2, 1536, 512], P(None, 'node', 'hid')
- edge_second_copy: bfloat16 [2, 512, 512], P(None, 'hid', 'node')
- node_first_copy: bfloat16 [2, 1024, 512], P(None, 'node', 'hid')
- node_second_copy: bfloat16 [2, 512, 512], P(None, 'hid', 'node')
- small_new: float32 [2, 8, 512], replicated
- small_m_new: float32 [2, 8, 512], replicated
- small_v_new: float32 [2, 8, 512], replicated
- norms: float32 [2, 12, 2], replicated
Inputs may be any that keep to these rules, and one draw needn't show every extreme that they name: `recv_local`: within each block of 1280 edges the values never fall, and every one of the block's 160 nodes receives at least one edge. `send_slot`: below 160: a node of the edge's own block; 160 to 199: an entry of the previous block's list; above: an entry of the next block's list. `halo_lists`: row 2b holds 40 different nodes of block b, numbered within the block, read by the previous block; row 2b + 1 those read by the next block.
All inputs are finite; a program needn't handle non-finite values. No bound on the sum of `ocean_mask` or of `present_mask` on one device may be relied on, other than what follows from the above.
Results may differ from a plain program's by a relative error of at most 0.023.
Values may be sent and summed in bfloat16 or wider, within the bound.
No kernel may reach another device: no remote copies, remote signals or barrier semaphores. Data moves between devices by JAX's collectives and lax.ppermute only.
A program may use at most 256 MiB of HBM per device.

v0:
```python
import jax
import jax.numpy as jnp
from jax import lax
from jax.sharding import PartitionSpec as P

LAYERS = 2


NORM_EPS = 1e-05
BETA_FIRST = 0.5
BETA_SECOND = 0.5
ADAM_EPS = 1e-06
WEIGHT_DECAY = 0.01


def extended(block, sides, width):
    for axis, dim in sides:
        count = lax.axis_size(axis)
        forward = [(i, i + 1) for i in range(count - 1)]
        forward.append((count - 1, 0))
        backward = [(target, source) for source, target in forward]
        low = lax.ppermute(
            lax.slice_in_dim(block, block.shape[dim] - width, None, axis=dim), axis, forward
        )
        high = lax.ppermute(lax.slice_in_dim(block, 0, width, axis=dim), axis, backward)
        block = jnp.concatenate([low, block, high], axis=dim)
    return block


def silu_slope(values):
    sigmoid = jax.nn.sigmoid(values)
    return sigmoid * (1.0 + values * (1.0 - sigmoid))


def norm_forward(values, gain_row, shift_row):
    center = values - jnp.mean(values, axis=-1, keepdims=True)
    spread = jnp.mean(center * center, axis=-1, keepdims=True)
    inverse = lax.rsqrt(spread + NORM_EPS)
    normed = center * inverse
    return (normed * gain_row + shift_row, normed, inverse)


def norm_backward(upstream, normed, inverse, gain_row):
    scaled = upstream * gain_row
    values_grad = inverse * (
        scaled
        - jnp.mean(scaled, axis=-1, keepdims=True)
        - normed * jnp.mean(scaled * normed, axis=-1, keepdims=True)
    )
    return (values_grad, jnp.sum(upstream * normed, axis=(0, 1)), jnp.sum(upstream, axis=(0, 1)))


def reduce_rows(active, second_weight):
    return lax.psum_scatter(
        jnp.einsum("rsh,hl->rsl", active, second_weight, preferred_element_type=jnp.float32).astype(
            jnp.bfloat16
        ),
        "hid",
        scatter_dimension=0,
        tiled=True,
    ).astype(jnp.float32)


def collect_grads(term_rows, total_rows):
    return lax.psum_scatter(
        term_rows(jnp.int32(0), total_rows // lax.axis_size("hid") * lax.axis_size("hid")).astype(
            jnp.bfloat16
        ),
        "hid",
        scatter_dimension=0,
        tiled=True,
    ).astype(jnp.float32)


def spread_rows(values):
    return lax.all_gather(values, "hid", axis=0, tiled=True)


def spread_grads(values):
    return lax.all_gather(values, "hid", axis=0, tiled=True)


def fetch_senders(rows, halo_width):
    return extended(rows, (("node", 0),), halo_width)


def return_senders(rows, halo_width):
    return extended(rows.astype(jnp.bfloat16), (("node", 0),), halo_width).astype(rows.dtype)


def column_slice(vector, hid_index, hid_width):
    return lax.dynamic_slice_in_dim(vector, hid_index * hid_width, hid_width, 0)


def adam_terms(weight, grad, first, second, decay):
    first_new = BETA_FIRST * first + (1.0 - BETA_FIRST) * grad
    second_new = BETA_SECOND * second + (1.0 - BETA_SECOND) * grad * grad
    update = first_new / (jnp.sqrt(second_new) + ADAM_EPS) + decay * weight
    return (first_new, second_new, update)


def target_rows(cotangent, ocean_mask, present_mask, valid_counts, node_total):
    valid_mask = (ocean_mask[:, None] * present_mask).astype(jnp.float32)
    scaling = node_total * lax.axis_size("node") / valid_counts.astype(jnp.float32)
    return cotangent.astype(jnp.float32) * valid_mask[:, :, None] * scaling[None, :, None]


def hidden_pass(
    node_in,
    edge_in,
    cotangent,
    ocean_mask,
    present_mask,
    valid_counts,
    send_slot,
    recv_local,
    halo_lists,
    small_params,
    edge_one,
    edge_two,
    node_one,
    node_two,
):
    hid_count = lax.axis_size("hid")
    hid_index = lax.axis_index("hid")
    node_total = node_in.shape[0]
    edge_total = edge_in.shape[0]
    sample_count = node_in.shape[1]
    latent = edge_in.shape[1]
    node_part = node_total // hid_count
    edge_part = edge_total // hid_count
    hid_width = edge_one.shape[2]
    halo_width = halo_lists.shape[1]
    halo_flat = halo_lists.reshape(-1)
    node_state = lax.dynamic_slice_in_dim(node_in, hid_index * node_part, node_part, 0).astype(
        jnp.float32
    )
    edge_state = lax.dynamic_slice_in_dim(edge_in, hid_index * edge_part, edge_part, 0).astype(
        jnp.float32
    )[:, None, :]
    node_low = node_in
    edge_low = edge_in
    stashed = []
    for depth in range(LAYERS):
        params = small_params[depth]
        first_edge = edge_one[depth]
        own_weight = first_edge[:latent]
        send_weight = first_edge[latent : 2 * latent]
        recv_weight = first_edge[2 * latent :]
        arrived = fetch_senders(node_low[halo_flat], halo_width)
        sender_table = jnp.concatenate(
            [node_low, arrived[:halo_width], arrived[3 * halo_width :]], axis=0
        )
        sender_proj = jnp.einsum(
            "tsl,lh->tsh", sender_table, send_weight, preferred_element_type=jnp.float32
        )
        receiver_proj = jnp.einsum(
            "nsl,lh->nsh", node_low, recv_weight, preferred_element_type=jnp.float32
        )
        if depth == 0:
            own_proj = jnp.einsum(
                "el,lh->eh", edge_low, own_weight, preferred_element_type=jnp.float32
            )[:, None, :]
        else:
            own_proj = jnp.einsum(
                "esl,lh->esh", edge_low, own_weight, preferred_element_type=jnp.float32
            )
        edge_pre = (
            own_proj
            + sender_proj[send_slot]
            + receiver_proj[recv_local]
            + column_slice(params[0], hid_index, hid_width)
        )
        edge_act = jax.nn.silu(edge_pre).astype(jnp.bfloat16)
        edge_sum = reduce_rows(edge_act, edge_two[depth]) + params[1]
        edge_update, edge_normed, edge_inverse = norm_forward(edge_sum, params[2], params[3])
        edge_state = edge_state + edge_update
        edge_full = spread_rows(edge_state.astype(jnp.bfloat16))
        pooled = jax.ops.segment_sum(
            edge_full.astype(jnp.float32),
            recv_local,
            num_segments=node_total,
            indices_are_sorted=True,
        )
        pooled_low = pooled.astype(jnp.bfloat16)
        first_node = node_one[depth]
        node_pre = (
            jnp.einsum(
                "nsl,lh->nsh", node_low, first_node[:latent], preferred_element_type=jnp.float32
            )
            + jnp.einsum(
                "nsl,lh->nsh", pooled_low, first_node[latent:], preferred_element_type=jnp.float32
            )
            + column_slice(params[4], hid_index, hid_width)
        )
        node_act = jax.nn.silu(node_pre).astype(jnp.bfloat16)
        node_sum = reduce_rows(node_act, node_two[depth]) + params[5]
        node_update, node_normed, node_inverse = norm_forward(node_sum, params[6], params[7])
        node_state = node_state + node_update
        stashed.append(
            (
                node_low,
                sender_table,
                edge_low,
                edge_pre,
                edge_act,
                edge_normed,
                edge_inverse,
                pooled_low,
                node_pre,
                node_act,
                node_normed,
                node_inverse,
            )
        )
        if depth < LAYERS - 1:
            node_low = spread_rows(node_state.astype(jnp.bfloat16))
            edge_low = edge_full
    node_out = node_state.astype(jnp.bfloat16)
    node_grad = target_rows(cotangent, ocean_mask, present_mask, valid_counts, node_total)
    edge_grad = jnp.zeros((edge_part, sample_count, latent), jnp.float32)
    carried = None
    edge_input_grad = None
    first_edge_grads = [None] * LAYERS
    second_edge_grads = [None] * LAYERS
    first_node_grads = [None] * LAYERS
    second_node_grads = [None] * LAYERS
    minor_grads = [None] * LAYERS
    zero_row = jnp.zeros((latent,), jnp.float32)
    for depth in reversed(range(LAYERS)):
        (
            node_low,
            sender_table,
            edge_low,
            edge_pre,
            edge_act,
            edge_normed,
            edge_inverse,
            pooled_low,
            node_pre,
            node_act,
            node_normed,
            node_inverse,
        ) = stashed[depth]
        params = small_params[depth]
        first_edge = edge_one[depth]
        first_node = node_one[depth]
        node_sum_grad, node_gain_grad, node_shift_grad = norm_backward(
            node_grad, node_normed, node_inverse, params[6]
        )
        node_sum_low = node_sum_grad.astype(jnp.bfloat16)
        node_bias_two = jnp.sum(node_sum_low.astype(jnp.float32), axis=(0, 1))
        node_full_grad = spread_grads(node_sum_low)
        node_act_grad = jnp.einsum(
            "nsl,hl->nsh", node_full_grad, node_two[depth], preferred_element_type=jnp.float32
        )
        second_node_grads[depth] = jnp.einsum(
            "nsh,nsl->hl", node_act, node_full_grad, preferred_element_type=jnp.float32
        )
        node_pre_grad = (node_act_grad * silu_slope(node_pre)).astype(jnp.bfloat16)
        node_bias_one = jnp.sum(node_pre_grad.astype(jnp.float32), axis=(0, 1))
        first_node_grads[depth] = jnp.concatenate(
            [
                jnp.einsum(
                    "nsl,nsh->lh", node_low, node_pre_grad, preferred_element_type=jnp.float32
                ),
                jnp.einsum(
                    "nsl,nsh->lh", pooled_low, node_pre_grad, preferred_element_type=jnp.float32
                ),
            ],
            axis=0,
        )
        node_input_grad = jnp.einsum(
            "nsh,lh->nsl", node_pre_grad, first_node[:latent], preferred_element_type=jnp.float32
        )
        pooled_grad = jnp.einsum(
            "nsh,lh->nsl", node_pre_grad, first_node[latent:], preferred_element_type=jnp.float32
        )

        def edge_rows_grad(first_row, row_count, pooled_grad=pooled_grad, carried=carried):
            term_rows = pooled_grad[recv_local]
            if carried is not None:
                later_grad, later_weight = carried
                term_rows = term_rows + jnp.einsum(
                    "esh,lh->esl", later_grad, later_weight, preferred_element_type=jnp.float32
                )
            return term_rows

        edge_grad = edge_grad + collect_grads(edge_rows_grad, edge_total)
        edge_sum_grad, edge_gain_grad, edge_shift_grad = norm_backward(
            edge_grad, edge_normed, edge_inverse, params[2]
        )
        edge_sum_low = edge_sum_grad.astype(jnp.bfloat16)
        edge_bias_two = jnp.sum(edge_sum_low.astype(jnp.float32), axis=(0, 1))
        edge_full_grad = spread_grads(edge_sum_low)
        edge_act_grad = jnp.einsum(
            "esl,hl->esh", edge_full_grad, edge_two[depth], preferred_element_type=jnp.float32
        )
        second_edge_grads[depth] = jnp.einsum(
            "esh,esl->hl", edge_act, edge_full_grad, preferred_element_type=jnp.float32
        )
        edge_pre_grad = (edge_act_grad * silu_slope(edge_pre)).astype(jnp.bfloat16)
        edge_bias_one = jnp.sum(edge_pre_grad.astype(jnp.float32), axis=(0, 1))
        own_weight = first_edge[:latent]
        send_weight = first_edge[latent : 2 * latent]
        recv_weight = first_edge[2 * latent :]
        if depth == 0:
            own_grad = jnp.einsum(
                "el,esh->lh", edge_low, edge_pre_grad, preferred_element_type=jnp.float32
            )
        else:
            own_grad = jnp.einsum(
                "esl,esh->lh", edge_low, edge_pre_grad, preferred_element_type=jnp.float32
            )
        send_grad = jnp.einsum(
            "esl,esh->lh",
            sender_table[send_slot],
            edge_pre_grad,
            preferred_element_type=jnp.float32,
        )
        recv_grad = jnp.einsum(
            "esl,esh->lh", node_low[recv_local], edge_pre_grad, preferred_element_type=jnp.float32
        )
        first_edge_grads[depth] = jnp.concatenate([own_grad, send_grad, recv_grad], axis=0)
        send_back = jnp.einsum(
            "esh,lh->esl", edge_pre_grad, send_weight, preferred_element_type=jnp.float32
        )
        table_grad = jax.ops.segment_sum(
            send_back, send_slot, num_segments=node_total + 2 * halo_width
        )
        recv_back = jnp.einsum(
            "esh,lh->esl", edge_pre_grad, recv_weight, preferred_element_type=jnp.float32
        )
        node_input_grad = (
            node_input_grad
            + table_grad[:node_total]
            + jax.ops.segment_sum(
                recv_back, recv_local, num_segments=node_total, indices_are_sorted=True
            )
        )
        returned = return_senders(table_grad[node_total:], halo_width)
        node_input_grad = node_input_grad.at[halo_flat].add(
            jnp.concatenate([returned[:halo_width], returned[3 * halo_width :]], axis=0)
        )

        def node_rows_grad(first_row, row_count, node_input_grad=node_input_grad):
            return node_input_grad

        node_grad = node_grad + collect_grads(node_rows_grad, node_total)
        if depth > 0:
            carried = (edge_pre_grad, own_weight)
        else:

            def input_rows_grad(
                first_row, row_count, edge_pre_grad=edge_pre_grad, own_weight=own_weight
            ):
                return jnp.einsum(
                    "esh,lh->el", edge_pre_grad, own_weight, preferred_element_type=jnp.float32
                )

            edge_input_grad = jnp.sum(edge_grad, axis=1) + collect_grads(
                input_rows_grad, edge_total
            )
        minor_grads[depth] = jnp.stack(
            [
                lax.dynamic_update_slice_in_dim(zero_row, edge_bias_one, hid_index * hid_width, 0),
                edge_bias_two,
                edge_gain_grad,
                edge_shift_grad,
                lax.dynamic_update_slice_in_dim(zero_row, node_bias_one, hid_index * hid_width, 0),
                node_bias_two,
                node_gain_grad,
                node_shift_grad,
            ]
        )
    grads = (
        jnp.stack(first_edge_grads),
        jnp.stack(second_edge_grads),
        jnp.stack(first_node_grads),
        jnp.stack(second_node_grads),
    )
    return (node_out, node_grad, edge_input_grad, grads, jnp.stack(minor_grads))


def per_device(
    node_in,
    edge_in,
    cotangent,
    ocean_mask,
    present_mask,
    valid_counts,
    send_slot,
    recv_local,
    halo_lists,
    edge_first,
    edge_second,
    node_first,
    node_second,
    edge_first_m,
    edge_second_m,
    node_first_m,
    node_second_m,
    edge_first_v,
    edge_second_v,
    node_first_v,
    node_second_v,
    small_params,
    small_m,
    small_v,
    learn_rate,
):
    masters = (edge_first, edge_second, node_first, node_second)
    edge_one, edge_two, node_one, node_two = (
        lax.all_gather(edge_first.astype(jnp.bfloat16), "node", axis=1, tiled=True),
        lax.all_gather(edge_second.astype(jnp.bfloat16), "node", axis=2, tiled=True),
        lax.all_gather(node_first.astype(jnp.bfloat16), "node", axis=1, tiled=True),
        lax.all_gather(node_second.astype(jnp.bfloat16), "node", axis=2, tiled=True),
    )
    node_out, node_grad, edge_input_grad, grads, minor_local = hidden_pass(
        node_in,
        edge_in,
        cotangent,
        ocean_mask,
        present_mask,
        valid_counts,
        send_slot,
        recv_local,
        halo_lists,
        small_params,
        edge_one,
        edge_two,
        node_one,
        node_two,
    )
    reduced = (
        lax.psum_scatter(grads[0], "node", scatter_dimension=1, tiled=True),
        lax.psum_scatter(grads[1], "node", scatter_dimension=2, tiled=True),
        lax.psum_scatter(grads[2], "node", scatter_dimension=1, tiled=True),
        lax.psum_scatter(grads[3], "node", scatter_dimension=2, tiled=True),
    )
    minor_total = lax.psum(minor_local, ("node", "hid"))
    firsts = (edge_first_m, edge_second_m, node_first_m, node_second_m)
    seconds = (edge_first_v, edge_second_v, node_first_v, node_second_v)
    moment_list = []
    for position in range(4):
        moment_list.append(
            adam_terms(
                masters[position],
                reduced[position],
                firsts[position],
                seconds[position],
                WEIGHT_DECAY,
            )
        )
    update_local = jnp.stack(
        [jnp.sum(entry[2] * entry[2], axis=(1, 2)) for entry in moment_list], axis=1
    )
    weight_local = jnp.stack([jnp.sum(matrix * matrix, axis=(1, 2)) for matrix in masters], axis=1)
    weight_squares, update_squares = lax.psum((weight_local, update_local), ("node", "hid"))
    weight_norm = jnp.sqrt(weight_squares)
    update_norm = jnp.sqrt(update_squares)
    new_weights = []
    for position in range(4):
        ratio = weight_norm[:, position] / update_norm[:, position]
        new_weights.append(
            masters[position] - learn_rate[0] * ratio[:, None, None] * moment_list[position][2]
        )
    small_first, small_second, small_update = adam_terms(
        small_params, minor_total, small_m, small_v, 0.0
    )
    small_wnorm = jnp.sqrt(jnp.sum(small_params * small_params, axis=2))
    small_unorm = jnp.sqrt(jnp.sum(small_update * small_update, axis=2))
    small_new = (
        small_params - learn_rate[0] * (small_wnorm / small_unorm)[:, :, None] * small_update
    )
    norms = jnp.stack(
        [
            jnp.concatenate([weight_norm, small_wnorm], axis=1),
            jnp.concatenate([update_norm, small_unorm], axis=1),
        ],
        axis=2,
    )
    return (
        node_out,
        node_grad.astype(jnp.bfloat16),
        edge_input_grad.astype(jnp.bfloat16),
        new_weights[0],
        new_weights[1],
        new_weights[2],
        new_weights[3],
        moment_list[0][0],
        moment_list[1][0],
        moment_list[2][0],
        moment_list[3][0],
        moment_list[0][1],
        moment_list[1][1],
        moment_list[2][1],
        moment_list[3][1],
        new_weights[0].astype(jnp.bfloat16),
        new_weights[1].astype(jnp.bfloat16),
        new_weights[2].astype(jnp.bfloat16),
        new_weights[3].astype(jnp.bfloat16),
        small_new,
        small_first,
        small_second,
        norms,
    )


def solution(mesh):
    in_specs = (
        P("node", None, None),
        P("node", None),
        P(("node", "hid"), None, None),
        P(("node", "hid")),
        P(("node", "hid"), None),
        P(),
        P("node"),
        P("node"),
        P("node", None),
        P(None, "node", "hid"),
        P(None, "hid", "node"),
        P(None, "node", "hid"),
        P(None, "hid", "node"),
        P(None, "node", "hid"),
        P(None, "hid", "node"),
        P(None, "node", "hid"),
        P(None, "hid", "node"),
        P(None, "node", "hid"),
        P(None, "hid", "node"),
        P(None, "node", "hid"),
        P(None, "hid", "node"),
        P(),
        P(),
        P(),
        P(),
    )
    out_specs = (
        P(("node", "hid"), None, None),
        P(("node", "hid"), None, None),
        P(("node", "hid"), None),
        P(None, "node", "hid"),
        P(None, "hid", "node"),
        P(None, "node", "hid"),
        P(None, "hid", "node"),
        P(None, "node", "hid"),
        P(None, "hid", "node"),
        P(None, "node", "hid"),
        P(None, "hid", "node"),
        P(None, "node", "hid"),
        P(None, "hid", "node"),
        P(None, "node", "hid"),
        P(None, "hid", "node"),
        P(None, "node", "hid"),
        P(None, "hid", "node"),
        P(None, "node", "hid"),
        P(None, "hid", "node"),
        P(),
        P(),
        P(),
        P(),
    )
    return jax.shard_map(
        per_device, mesh=mesh, in_specs=in_specs, out_specs=out_specs, check_vma=False
    )
```

profile of v0, /device:TPU:0, one launch (start us, length us, event | category | flops | bytes accessed | tf_op | source)
XLA Modules:
  0.0 2155.9 jit_solution(12583336990937295041)
XLA Ops:
  22.1 36.5 %all_gather.34 = bf16[2,1536,128]{2,1,0:T(8,128)(2,1)S(1)} all-gather(bf16[2,192,128]{2,1,0:T(8,128)(2,1)S(1)} %convert_element_type.196), channel_id=1, replica_groups=mesh['node'=8,'hid'=4] {'node'}, dimensions={1}, use_global_device_ids=true | all-gather | bytes 884736 | tf_op jit(solution)/shard_map/all_gather | solution.py:414
  61.4 30.8 %all_gather.35 = bf16[2,128,512]{1,0,2:T(2,128)(2,1)S(1)} all-gather(bf16[2,128,64]{1,0,2:T(2,128)(2,1)S(1)} %copy.478), channel_id=1, replica_groups=mesh['node'=8,'hid'=4] {'node'}, dimensions={2}, use_global_device_ids=true | all-gather | bytes 294912 | tf_op jit(solution)/shard_map/all_gather | solution.py:415
  122.0 65.4 %reduce-scatter.19.cloned.1.call-done = bf16[320,6,512]{2,0,1:T(8,128)(2,1)} async-done(((bf16[1280,6,512]{2,0,1:T(8,128)(2,1)}), bf16[320,6,512]{2,0,1:T(8,128)(2,1)}) %reduce-scatter.19.cloned.1.call-update) | async-done | bytes 1966096 | tf_op jit(solution)/shard_map/reduce_scatter | solution.py:54
  194.3 30.9 %all_gather.37 = bf16[2,128,512]{1,0,2:T(2,128)(2,1)S(1)} all-gather(bf16[2,128,64]{1,0,2:T(2,128)(2,1)S(1)} %copy.477), channel_id=1, replica_groups=mesh['node'=8,'hid'=4] {'node'}, dimensions={2}, use_global_device_ids=true | all-gather | bytes 294912 | tf_op jit(solution)/shard_map/all_gather | solution.py:417
  230.3 31.2 %all_gather.33 = bf16[2,1024,128]{2,1,0:T(8,128)(2,1)S(1)} all-gather(bf16[2,128,128]{2,1,0:T(8,128)(2,1)S(1)} %get-tuple-element.196), channel_id=1, replica_groups=mesh['node'=8,'hid'=4] {'node'}, dimensions={1}, use_global_device_ids=true | all-gather | bytes 589824 | tf_op jit(solution)/shard_map/all_gather | solution.py:416
  263.5 12.8 copy.282
  278.1 170.8 %scatter_fusion = f32[160,6,512]{2,1,0:T(8,128)} fusion(f32[160,6,512]{2,1,0:T(8,128)} %broadcast.231.clone, s32[1280]{0:T(1024)S(1)} %copy-done.82, f32[1280,6,512]{2,1,0:T(8,128)} %copy.282), kind=kCustom, calls=%fused_computation.12 | custom fusion | flops 3932160 | bytes 47191040 | tf_op jit(solution)/shard_map/scatter-add | solution.py:179
  456.6 23.5 %reduce-scatter.31.cloned.1.call-done = bf16[40,3072]{1,0:T(8,128)(2,1)} async-done(((bf16[160,3072]{1,0:T(8,128)(2,1)}), bf16[40,3072]{1,0:T(8,128)(2,1)}) %reduce-scatter.31.cloned.1.call-update) | async-done | bytes 245776
  539.1 66.4 %reduce-scatter.21.cloned.1.call-done = bf16[320,6,512]{2,0,1:T(8,128)(2,1)} async-done(((bf16[1280,6,512]{2,0,1:T(8,128)(2,1)}), bf16[320,6,512]{2,0,1:T(8,128)(2,1)}) %reduce-scatter.21.cloned.1.call-update) | async-done | bytes 1966096 | tf_op jit(solution)/shard_map/reduce_scatter | solution.py:54
  618.6 51.7 %all-gather.7.cloned.1.call-done = bf16[1280,6,512]{2,0,1:T(8,128)(2,1)} async-done(((bf16[320,6,512]{2,0,1:T(8,128)(2,1)}), bf16[1280,6,512]{2,0,1:T(8,128)(2,1)}) %all-gather.7.cloned.1.call-update) | async-done | bytes 7864336 | tf_op jit(solution)/shard_map/all_gather | solution.py:76
  670.3 12.8 copy.294
  683.4 112.6 %scatter_fusion.1 = f32[160,6,512]{2,1,0:T(8,128)S(1)} fusion(f32[160,6,512]{2,1,0:T(8,128)S(1)} %broadcast.231, s32[1280]{0:T(1024)S(1)} %copy-done.83, f32[1280,6,512]{2,1,0:T(8,128)} %copy.294), kind=kCustom, calls=%fused_computation.13 | custom fusion | flops 3932160 | bytes 47191040 | tf_op jit(solution)/shard_map/scatter-add | solution.py:179
  801.8 24.4 %reduce-scatter.33.cloned.1.call-done = bf16[40,3072]{1,0:T(8,128)(2,1)} async-done(((bf16[160,3072]{1,0:T(8,128)(2,1)}), bf16[40,3072]{1,0:T(8,128)(2,1)}) %reduce-scatter.33.cloned.1.call-update) | async-done | bytes 245776
  851.1 9.9 copy.476
  861.3 68.5 %reduce-scatter.23.cloned.1.call-done = bf16[320,6,512]{2,0,1:T(8,128)(2,1)} async-done(((bf16[1280,6,512]{2,0,1:T(8,128)(2,1)}), bf16[320,6,512]{2,0,1:T(8,128)(2,1)}) %reduce-scatter.23.cloned.1.call-update) | async-done | bytes 1966096 | tf_op jit(solution)/shard_map/reduce_scatter | solution.py:65
  938.0 55.4 %all-gather.9.cloned.1.call-done = bf16[1280,6,512]{2,0,1:T(8,128)(2,1)} async-done(((bf16[320,6,512]{2,0,1:T(8,128)(2,1)}), bf16[1280,6,512]{2,0,1:T(8,128)(2,1)}) %all-gather.9.cloned.1.call-update) | async-done | bytes 7864336 | tf_op jit(solution)/shard_map/all_gather | solution.py:80
  1003.7 28.5 %copy.299 = f32[1280,6,512]{2,1,0:T(8,128)} copy(f32[1280,6,512]{2,0,1:T(8,128)S(1)} %fusion.76) | data formatting | bytes 31457280 | tf_op jit(solution)/shard_map/esh,lh->esl/dot_general | solution.py:325
  1034.6 167.8 %scatter_fusion.2 = f32[240,6,512]{2,1,0:T(8,128)} fusion(f32[240,6,512]{2,1,0:T(8,128)} %broadcast.242.clone, s32[1280]{0:T(1024)S(1)} %copy-done.107, f32[1280,6,512]{2,1,0:T(8,128)} %copy.299), kind=kCustom, calls=%fused_computation.14 | custom fusion | flops 3932160 | bytes 47191040 | tf_op jit(solution)/shard_map/scatter-add | solution.py:328
  1219.4 28.3 %copy.302 = f32[1280,6,512]{2,1,0:T(8,128)} copy(f32[1280,6,512]{2,0,1:T(8,128)S(1)} %fusion.78) | data formatting | bytes 31457280 | tf_op jit(solution)/shard_map/esh,lh->esl/dot_general | solution.py:331
  1247.7 171.3 %scatter_fusion.3 = f32[160,6,512]{2,1,0:T(8,128)} fusion(f32[160,6,512]{2,1,0:T(8,128)} %copy.301, s32[1280]{0:T(1024)S(1)} %copy-done.83, f32[1280,6,512]{2,1,0:T(8,128)} %copy.302), kind=kCustom, calls=%fused_computation.15 | custom fusion | flops 3932160 | bytes 47191040 | tf_op jit(solution)/shard_map/scatter-add | solution.py:337
  1421.5 11.1 scatter_fusion.4
  1436.7 22.7 %reduce-scatter.35.cloned.1.call-done = bf16[40,3072]{1,0:T(8,128)(2,1)} async-done(((bf16[160,3072]{1,0:T(8,128)(2,1)}), bf16[40,3072]{1,0:T(8,128)(2,1)}) %reduce-scatter.35.cloned.1.call-update) | async-done | bytes 245776
  1479.8 11.6 gather_fusion.7
  1491.4 18.3 fusion
  1509.8 68.7 %reduce-scatter.25.cloned.1.call-done = bf16[320,6,512]{2,0,1:T(8,128)(2,1)} async-done(((bf16[1280,6,512]{2,0,1:T(8,128)(2,1)}), bf16[320,6,512]{2,0,1:T(8,128)(2,1)}) %reduce-scatter.25.cloned.1.call-update) | async-done | bytes 1966096 | tf_op jit(solution)/shard_map/reduce_scatter | solution.py:65
  1588.1 26.8 %gather_fusion.9 = bf16[1280,6,512]{2,0,1:T(8,128)(2,1)} fusion(bf16[160,6,512]{2,0,1:T(8,128)(2,1)S(1)} %copy-done.1, s32[2048]{0:T(1024)S(1)} %copy-done.68), kind=kCustom, calls=%fused_computation.9 | custom fusion | bytes 15733760 | tf_op jit(solution)/shard_map/gather | solution.py:322
  1675.6 9.8 convert_reduce_fusion.1
  1710.3 28.1 %copy.306 = f32[1280,6,512]{2,1,0:T(8,128)} copy(f32[1280,6,512]{2,0,1:T(8,128)S(1)} %fusion.69) | data formatting | bytes 31457280 | tf_op jit(solution)/shard_map/esh,lh->esl/dot_general | solution.py:325
  1740.9 168.3 %scatter_fusion.5 = f32[240,6,512]{2,1,0:T(8,128)} fusion(f32[240,6,512]{2,1,0:T(8,128)} %broadcast.242, s32[1280]{0:T(1024)S(1)} %copy-done.108, f32[1280,6,512]{2,1,0:T(8,128)} %copy.306), kind=kCustom, calls=%fused_computation.17 | custom fusion | flops 3932160 | bytes 47191040 | tf_op jit(solution)/shard_map/scatter-add | solution.py:328
  1924.8 28.3 %copy.309 = f32[1280,6,512]{2,1,0:T(8,128)} copy(f32[1280,6,512]{2,0,1:T(8,128)S(1)} %fusion.71) | data formatting | bytes 31457280 | tf_op jit(solution)/shard_map/esh,lh->esl/dot_general | solution.py:331
  1953.1 112.6 %scatter_fusion.6 = f32[160,6,512]{2,1,0:T(8,128)S(1)} fusion(f32[160,6,512]{2,1,0:T(8,128)S(1)} %copy.308, s32[1280]{0:T(1024)S(1)} %copy-done.84, f32[1280,6,512]{2,1,0:T(8,128)} %copy.309), kind=kCustom, calls=%fused_computation.18 | custom fusion | flops 3932160 | bytes 47191040 | tf_op jit(solution)/shard_map/scatter-add | solution.py:337
  2101.9 39.6 %all-reduce.3 = (f32[2,4]{0,1:T(4,128)S(1)}, f32[2,4]{0,1:T(4,128)S(1)}, f32[2,8,512]{2,1,0:T(8,128)S(1)}) all-reduce(f32[2,4]{0,1:T(4,128)S(1)} %pad_maximum_fusion.12, f32[2,4]{0,1:T(4,128)S(1)} %pad_maximum_fusion.11, f32[2,8,512]{2,1,0:T(8,128)S(1)} %pad_maximum_fusion.10), channel_id=1, replica_groups=mesh['node'=8,'hid'=4] {'node','hid'}, use_global_device_ids=true, to_apply=%region_48.49 | all-reduce | flops 8208 | bytes 65664 | tf_op jit(solution)/shard_map/psum | solution.py:459
  (583 shorter events, 391.9 us)
Async XLA Ops:
  7.2 180.2 %reduce-scatter.19.cloned.1.call-start = ((), (), s32[]{:S(2)}) async-start(), calls=%async_computation.10 | async-start | bytes 9830400 | tf_op jit(solution)/shard_map/reduce_scatter | solution.py:54
  15.5 83.1 %collective-permute-start = (bf16[40,6,512]{2,0,1:T(8,128)(2,1)}, bf16[40,6,512]{2,0,1:T(8,128)(2,1)}, u32[]{:S(2)}, u32[]{:S(2)}) collective-permute-start(bf16[40,6,512]{2,0,1:T(8,128)(2,1)} %get-tuple-element.189), channel_id=1, source_target_pairs={{0,4},{4,8},{8,12},{12,16},{16,20},{20,24},{24,28},{28,0},{1,5},{5... | collective-permute-start | bytes 737288 | tf_op jit(solution)/shard_map/ppermute | solution.py:22
  18.4 81.1 %collective-permute-start.1 = (bf16[40,6,512]{2,0,1:T(8,128)(2,1)}, bf16[40,6,512]{2,0,1:T(8,128)(2,1)}, u32[]{:S(2)}, u32[]{:S(2)}) collective-permute-start(bf16[40,6,512]{2,0,1:T(8,128)(2,1)} %get-tuple-element.188), channel_id=1, source_target_pairs={{4,0},{8,4},{12,8},{16,12},{20,16},{24,20},{28,24},{0,28},{5,1},{9... | collective-permute-start | bytes 737288 | tf_op jit(solution)/shard_map/ppermute | solution.py:25
  22.1 170.0 %copy-start.111 = (f32[1,1,512]{2,1,0:T(1,128)}, f32[1,1,512]{2,1,0:T(1,128)S(1)}, u32[]{:S(2)}) copy-start(f32[1,1,512]{2,1,0:T(1,128)S(1)} %get-tuple-element.210) | copy-start | bytes 6148
  22.1 170.0 %copy-start.121 = (f32[1,1,512]{2,1,0:T(1,128)}, f32[1,1,512]{2,1,0:T(1,128)S(1)}, u32[]{:S(2)}) copy-start(f32[1,1,512]{2,1,0:T(1,128)S(1)} %get-tuple-element.209) | copy-start | bytes 6148
  22.1 588.0 %copy-start.99 = (f32[1,1,512]{2,1,0:T(1,128)}, f32[1,1,512]{2,1,0:T(1,128)S(1)}, u32[]{:S(2)}) copy-start(f32[1,1,512]{2,1,0:T(1,128)S(1)} %get-tuple-element.211) | copy-start | bytes 6148
  119.8 143.7 %all-gather.5.cloned.1.call-start = ((), (), s32[]{:S(2)}) async-start(), calls=%async_computation.11 | async-start | bytes 9830400 | tf_op jit(solution)/shard_map/all_gather | solution.py:76
  189.6 420.5 %copy-start.65 = (f32[320,6]{0,1:T(8,128)}, f32[320,6]{0,1:T(8,128)S(1)}, u32[]{:S(2)}) copy-start(f32[320,6]{0,1:T(8,128)S(1)} %broadcast_multiply_fusion.5) | copy-start | bytes 23044
  194.2 285.8 %reduce-scatter.31.cloned.1.call-start = ((), (), s32[]{:S(2)}) async-start(), calls=%async_computation.20 | async-start | bytes 1228800
  454.6 150.9 %reduce-scatter.21.cloned.1.call-start = ((), (), s32[]{:S(2)}) async-start(), calls=%async_computation.12 | async-start | bytes 9830400 | tf_op jit(solution)/shard_map/reduce_scatter | solution.py:54
  497.6 15.1 collective-permute-start.2
  501.5 12.6 collective-permute-start.3
  539.0 131.2 %all-gather.7.cloned.1.call-start = ((), (), s32[]{:S(2)}) async-start(), calls=%async_computation.13 | async-start | bytes 9830400 | tf_op jit(solution)/shard_map/all_gather | solution.py:76
  614.8 211.4 %reduce-scatter.33.cloned.1.call-start = ((), (), s32[]{:S(2)}) async-start(), calls=%async_computation.21 | async-start | bytes 1228800
  801.6 128.1 %reduce-scatter.23.cloned.1.call-start = ((), (), s32[]{:S(2)}) async-start(), calls=%async_computation.14 | async-start | bytes 9830400 | tf_op jit(solution)/shard_map/reduce_scatter | solution.py:65
  801.7 660.6 %copy-start.126 = (f32[6]{0:T(128)}, f32[6]{0:T(128)S(1)}, u32[]{:S(2)}) copy-start(f32[6]{0:T(128)S(1)} %convert_divide_fusion) | copy-start | bytes 76
  801.7 660.6 %copy-start.91 = (f32[40,6]{0,1:T(8,128)}, f32[40,6]{0,1:T(8,128)S(1)}, u32[]{:S(2)}) copy-start(f32[40,6]{0,1:T(8,128)S(1)} %multiply_convert_fusion.7) | copy-start | bytes 2884
  861.0 132.3 %all-gather.9.cloned.1.call-start = ((), (), s32[]{:S(2)}) async-start(), calls=%async_computation.15 | async-start | bytes 9830400 | tf_op jit(solution)/shard_map/all_gather | solution.py:80
  937.9 521.5 %reduce-scatter.35.cloned.1.call-start = ((), (), s32[]{:S(2)}) async-start(), calls=%async_computation.22 | async-start | bytes 1228800
  1000.4 490.9 %copy-start.11 = (bf16[1280,6,128]{2,0,1:T(8,128)(2,1)}, bf16[1280,6,128]{2,0,1:T(8,128)(2,1)S(1)}, u32[]{:S(2)}) copy-start(bf16[1280,6,128]{2,0,1:T(8,128)(2,1)S(1)} %get-tuple-element.222) | copy-start | bytes 5898244
  1209.8 209.2 %collective-permute-start.4 = (bf16[40,6,512]{2,1,0:T(8,128)(2,1)}, bf16[40,6,512]{2,1,0:T(8,128)(2,1)}, u32[]{:S(2)}, u32[]{:S(2)}) collective-permute-start(bf16[40,6,512]{2,1,0:T(8,128)(2,1)} %get-tuple-element.180), channel_id=1, source_target_pairs={{0,4},{4,8},{8,12},{12,16},{16,20},{20,24},{24,28},{28,0},{1,5},{5... | collective-permute-start | bytes 737288 | tf_op jit(solution)/shard_map/ppermute | solution.py:22
  1211.2 207.8 %collective-permute-start.5 = (bf16[40,6,512]{2,1,0:T(8,128)(2,1)S(1)}, bf16[40,6,512]{2,1,0:T(8,128)(2,1)}, u32[]{:S(2)}, u32[]{:S(2)}) collective-permute-start(bf16[40,6,512]{2,1,0:T(8,128)(2,1)S(1)} %get-tuple-element.181), channel_id=1, source_target_pairs={{4,0},{8,4},{12,8},{16,12},{20,16},{24,20},{28,24},{0,28},{5,1},{9... | collective-permute-start | bytes 737288 | tf_op jit(solution)/shard_map/ppermute | solution.py:25
  1247.7 171.3 %slice-start.2 = ((bf16[240,6,512]{2,1,0:T(8,128)(2,1)}), bf16[80,6,512]{2,1,0:T(8,128)(2,1)S(1)}, s32[]{:S(2)}) async-start(bf16[240,6,512]{2,1,0:T(8,128)(2,1)} %copy-done.29), calls=%async_computation.27 | async-start | bytes 1310720 | tf_op jit(solution)/shard_map/slice | solution.py:341
  1436.6 141.9 %reduce-scatter.25.cloned.1.call-start = ((), (), s32[]{:S(2)}) async-start(), calls=%async_computation.16 | async-start | bytes 9830400 | tf_op jit(solution)/shard_map/reduce_scatter | solution.py:65
  1475.7 195.7 %copy-start.42 = (bf16[160,6,128]{2,0,1:T(8,128)(2,1)}, bf16[160,6,128]{2,0,1:T(8,128)(2,1)S(1)}, u32[]{:S(2)}) copy-start(bf16[160,6,128]{2,0,1:T(8,128)(2,1)S(1)} %get-tuple-element.226) | copy-start | bytes 737284
  1509.8 165.8 %all-gather.11.cloned.1.call-start = ((), (), s32[]{:S(2)}) async-start(), calls=%async_computation.17 | async-start | bytes 9830400 | tf_op jit(solution)/shard_map/all_gather | solution.py:80
  1588.0 497.6 %reduce-scatter.29.cloned.1.call-start = ((), (), s32[]{:S(2)}) async-start(), calls=%async_computation.19 | async-start | bytes 1179648 | tf_op jit(solution)/shard_map/reduce_scatter | solution.py:438
  1675.5 414.7 %all-reduce.7.cloned.1.call-start = ((), (), s32[]{:S(2)}) async-start(), calls=%async_computation.24 | async-start | bytes 5242880
  1707.9 392.1 %reduce-scatter.37.cloned.1.call-start = ((), (), s32[]{:S(2)}) async-start(), calls=%async_computation.23 | async-start | bytes 1228800
  1914.5 151.3 %collective-permute-start.6 = (bf16[40,6,512]{2,1,0:T(8,128)(2,1)}, bf16[40,6,512]{2,1,0:T(8,128)(2,1)}, u32[]{:S(2)}, u32[]{:S(2)}) collective-permute-start(bf16[40,6,512]{2,1,0:T(8,128)(2,1)} %get-tuple-element.178), channel_id=1, source_target_pairs={{0,4},{4,8},{8,12},{12,16},{16,20},{20,24},{24,28},{28,0},{1,5},{5... | collective-permute-start | bytes 737288 | tf_op jit(solution)/shard_map/ppermute | solution.py:22
  1915.9 149.9 %collective-permute-start.7 = (bf16[40,6,512]{2,1,0:T(8,128)(2,1)}, bf16[40,6,512]{2,1,0:T(8,128)(2,1)}, u32[]{:S(2)}, u32[]{:S(2)}) collective-permute-start(bf16[40,6,512]{2,1,0:T(8,128)(2,1)} %get-tuple-element.179), channel_id=1, source_target_pairs={{4,0},{8,4},{12,8},{16,12},{20,16},{24,20},{28,24},{0,28},{5,1},{9... | collective-permute-start | bytes 737288 | tf_op jit(solution)/shard_map/ppermute | solution.py:25
  2078.1 69.0 %reduce-scatter.27.cloned.1.call-start = ((), (), s32[]{:S(2)}) async-start(), calls=%async_computation.18 | async-start | bytes 1638400 | tf_op jit(solution)/shard_map/reduce_scatter | solution.py:65
  (149 other events, 3508.8 us)
Sparse Core Ops, SparseCore 0:
  120.0 67.3 reduce-scatter.18
  194.3 55.2 all-gather.4
  454.7 25.3 reduce-scatter.30
  539.1 66.3 reduce-scatter.20
  615.0 55.2 all-gather.6
  801.7 24.4 reduce-scatter.32
  861.1 68.5 reduce-scatter.22
  938.0 55.2 all-gather.8
  1436.7 22.5 reduce-scatter.34
  1509.9 68.5 reduce-scatter.24
  1588.1 55.2 all-gather.10
  1675.6 64.6 reduce-scatter.28
  1744.3 115.2 all-reduce.6
  2078.2 21.6 reduce-scatter.36
  2102.4 26.4 reduce-scatter.26
where the time goes:
time: 2180 us; the launch traced here: 2160 us
  other arithmetic  1000 us (46%)
  waiting for transfers between devices  451 us (21%)
  local copies, waits for them, and re-layouts  320 us (15%)
  blocking collectives  196 us (9%)
  matrix products  145 us (7%)
  starting transfers between devices  21.9 us (1%)
    scatter-add x2, other arithmetic, hidden_pass(): jax.ops.segment_sum(send_back, send_slot, num_segments=node_total + 2 * h...  336 us
    scatter-add x2, other arithmetic, hidden_pass(): jax.ops.segment_sum(recv_back, recv_local, num_segments=node_total, indic...  284 us
    scatter-add x2, other arithmetic, hidden_pass(): jax.ops.segment_sum(edge_full.astype(jnp.float32), recv_local, num_segmen...  283 us
    reduce_scatter x3, waiting for transfers between devices, collect_grads(): lax.psum_scatter(term_rows(jnp.int32(0), total_rows // lax.axis_size('hid...  137 us
    reduce_scatter x2, waiting for transfers between devices, reduce_rows(): lax.psum_scatter(jnp.einsum('rsh,hl->rsl', active, second_weight, preferr...  132 us
    unnamed x20, waiting for transfers between devices  74.5 us
    dot_general x2, local copies, waits for them, and re-layouts, hidden_pass(): jnp.einsum('esh,lh->esl', edge_pre_grad, send_weight, preferred_element_t...  56.7 us
    dot_general x2, local copies, waits for them, and re-layouts, hidden_pass(): jnp.einsum('esh,lh->esl', edge_pre_grad, recv_weight, preferred_element_t...  56.6 us
  transfers between devices with their start and end apart: 23, of which 11 were waited for; matrix products, arithmetic and copies ran while one was open for 35% of the time, Pallas kernels for 0%

commit v1 on v0

v1 whole, which is shorter than its diff:
```python
import jax
import jax.numpy as jnp
from jax import lax
from jax.sharding import PartitionSpec as P

LAYERS = 2


NORM_EPS = 1e-05
BETA_FIRST = 0.5
BETA_SECOND = 0.5
ADAM_EPS = 1e-06
WEIGHT_DECAY = 0.01
BF16 = jnp.bfloat16
F32 = jnp.float32


def dot(spec, left, right):
    return jnp.einsum(spec, left, right, preferred_element_type=F32)


def silu_slope(values):
    sigmoid = jax.nn.sigmoid(values)
    return sigmoid * (1.0 + values * (1.0 - sigmoid))


def norm_forward(values, gain_row, shift_row):
    center = values - jnp.mean(values, axis=-1, keepdims=True)
    spread = jnp.mean(center * center, axis=-1, keepdims=True)
    inverse = lax.rsqrt(spread + NORM_EPS)
    normed = center * inverse
    return (normed * gain_row + shift_row, normed, inverse)


def norm_backward(upstream, normed, inverse, gain_row):
    scaled = upstream * gain_row
    return inverse * (
        scaled
        - jnp.mean(scaled, axis=-1, keepdims=True)
        - normed * jnp.mean(scaled * normed, axis=-1, keepdims=True)
    )


def swap(values, axis, bit):
    count = lax.axis_size(axis)
    return lax.ppermute(values, axis, [(i, i ^ (1 << bit)) for i in range(count)])


def bits_of(axis):
    return lax.axis_size(axis).bit_length() - 1


def halve_sum(parts, axis):
    index = lax.axis_index(axis)
    for bit in range(bits_of(axis)):
        place = bits_of(axis) - 1 - bit
        own = (index >> bit) & 1
        sent = lax.dynamic_index_in_dim(parts, 1 - own, place, keepdims=False)
        kept = lax.dynamic_index_in_dim(parts, own, place, keepdims=False)
        parts = kept + swap(sent.astype(BF16), axis, bit).astype(F32)
    return parts


def double_up(part, axis):
    index = lax.axis_index(axis)
    for bit in reversed(range(bits_of(axis))):
        place = bits_of(axis) - 1 - bit
        own = (index >> bit) & 1
        other = swap(part, axis, bit)
        low = jnp.where(own == 0, part, other)
        high = jnp.where(own == 0, other, part)
        part = jnp.stack([low, high], axis=place)
    return part


def split_rows(values, axis):
    bits = bits_of(axis)
    samples, rows, width = values.shape
    shaped = values.reshape((samples,) + (2,) * bits + (rows >> bits, width))
    return jnp.moveaxis(shaped, 0, bits)


def join_rows(parts, axis):
    bits = bits_of(axis)
    moved = jnp.moveaxis(parts, bits, 0)
    return moved.reshape(moved.shape[0], -1, moved.shape[-1])


def sum_rows(values):
    return halve_sum(split_rows(values, "hid"), "hid")


def sum_rows_spread(values):
    return join_rows(double_up(sum_rows(values).astype(BF16), "hid"), "hid")


def sum_everywhere(values):
    for axis in ("hid", "node"):
        for bit in range(bits_of(axis)):
            values = values + swap(values, axis, bit)
    return values


def to_neighbours(rows, halo_width):
    count = lax.axis_size("node")
    onward = [(i, (i + 1) % count) for i in range(count)]
    back = [(target, source) for source, target in onward]
    from_previous = lax.ppermute(rows[:, halo_width:], "node", onward)
    from_next = lax.ppermute(rows[:, :halo_width], "node", back)
    return jnp.concatenate([from_previous, from_next], axis=1)


def adam_terms(weight, grad, first, second, decay):
    first_new = BETA_FIRST * first + (1.0 - BETA_FIRST) * grad
    second_new = BETA_SECOND * second + (1.0 - BETA_SECOND) * grad * grad
    update = first_new / (jnp.sqrt(second_new) + ADAM_EPS) + decay * weight
    return (first_new, second_new, update)


def gather_pair(first, second):
    packed = jnp.concatenate([first, second.T], axis=0).astype(BF16)
    rows = first.shape[0]
    whole = lax.all_gather(packed, ("node", "hid"), axis=0, tiled=True)
    nodes, hids = lax.axis_size("node"), lax.axis_size("hid")
    whole = whole.reshape(nodes, hids, packed.shape[0], packed.shape[1])
    whole = whole.transpose(0, 2, 1, 3).reshape(nodes, packed.shape[0], hids * packed.shape[1])
    return (
        whole[:, :rows].reshape(nodes * rows, -1),
        whole[:, rows:].reshape(nodes * (packed.shape[0] - rows), -1),
    )


def scatter_pair(first_grad, second_grad):
    nodes, hids = lax.axis_size("node"), lax.axis_size("hid")
    width = first_grad.shape[1] // hids
    packed = jnp.concatenate(
        [
            first_grad.astype(BF16).reshape(nodes, -1, hids, width),
            second_grad.astype(BF16).reshape(nodes, -1, hids, width),
        ],
        axis=1,
    )
    packed = packed.transpose(0, 2, 1, 3)
    own = lax.psum_scatter(
        packed.reshape(-1, width), ("node", "hid"), scatter_dimension=0, tiled=True
    ).astype(F32)
    rows = first_grad.shape[0] // nodes
    return own[:rows], own[rows:].T


def flat(values):
    return values.reshape(-1, values.shape[-1])


def per_device(
    node_in,
    edge_in,
    cotangent,
    ocean_mask,
    present_mask,
    valid_counts,
    send_slot,
    recv_local,
    halo_lists,
    edge_first,
    edge_second,
    node_first,
    node_second,
    edge_first_m,
    edge_second_m,
    node_first_m,
    node_second_m,
    edge_first_v,
    edge_second_v,
    node_first_v,
    node_second_v,
    small_params,
    small_m,
    small_v,
    learn_rate,
):
    masters = (edge_first, edge_second, node_first, node_second)
    hid_count = lax.axis_size("hid")
    hid_index = lax.axis_index("hid")
    node_total, sample_count, latent = node_in.shape
    edge_part = edge_in.shape[0] // hid_count
    node_part = node_total // hid_count
    halo_width = halo_lists.shape[1]
    table_total = node_total + 2 * halo_width

    edge_weights = [None] * LAYERS
    node_weights = [None] * LAYERS
    for depth in range(LAYERS):
        edge_weights[depth] = gather_pair(edge_first[depth], edge_second[depth])
        node_weights[depth] = gather_pair(node_first[depth], node_second[depth])

    def own_edges(values):
        return lax.dynamic_slice_in_dim(values, hid_index * edge_part, edge_part, 0)

    def own_nodes(values):
        return lax.dynamic_slice_in_dim(values, hid_index * node_part, node_part, 1)

    sender = own_edges(send_slot)
    receiver = own_edges(recv_local)
    at_receiver = (receiver[:, None] == jnp.arange(node_total)[None, :]).astype(BF16)
    at_sender = (sender[:, None] == jnp.arange(table_total)[None, :]).astype(BF16)
    at_both = jnp.concatenate([at_sender, at_receiver], axis=1)
    at_halo = (halo_lists.reshape(-1)[:, None] == jnp.arange(node_total)[None, :]).astype(BF16)

    valid_mask = (ocean_mask[:, None] * present_mask).astype(BF16)
    masked = jnp.transpose(cotangent * valid_mask[:, :, None], (1, 0, 2))
    target = join_rows(double_up(masked, "hid"), "hid").astype(F32)
    scaling = node_total * lax.axis_size("node") / valid_counts.astype(F32)
    target = target * scaling[:, None, None]

    node_low = jnp.transpose(node_in, (1, 0, 2))
    node_state = node_low.astype(F32)
    edge_low = own_edges(edge_in)
    edge_state = edge_low.astype(F32)[None]
    stashed = []
    for depth in range(LAYERS):
        params = small_params[depth]
        first_edge, second_edge = edge_weights[depth]
        own_weight = first_edge[:latent]
        send_weight = first_edge[latent : 2 * latent]
        recv_weight = first_edge[2 * latent :]
        halo_rows = dot("hn,snl->shl", at_halo, node_low).astype(BF16)
        table = jnp.concatenate([node_low, to_neighbours(halo_rows, halo_width)], axis=1)
        projected = jnp.concatenate(
            [
                dot("snl,lh->snh", table, send_weight).astype(BF16),
                dot("snl,lh->snh", node_low, recv_weight).astype(BF16),
            ],
            axis=1,
        )
        if depth == 0:
            own_proj = dot("el,lh->eh", edge_low, own_weight)[None]
        else:
            own_proj = dot("sel,lh->seh", edge_low, own_weight)
        edge_pre = own_proj + dot("en,snh->seh", at_both, projected) + params[0]
        edge_act = jax.nn.silu(edge_pre).astype(BF16)
        edge_sum = dot("seh,lh->sel", edge_act, second_edge) + params[1]
        edge_update, edge_normed, edge_inverse = norm_forward(edge_sum, params[2], params[3])
        edge_state = edge_state + edge_update
        edge_next = edge_state.astype(BF16)
        pooled = sum_rows_spread(dot("en,sel->snl", at_receiver, edge_next))
        first_node, second_node = node_weights[depth]
        node_pre = (
            dot("snl,lh->snh", node_low, first_node[:latent])
            + dot("snl,lh->snh", pooled, first_node[latent:])
            + params[4]
        )
        node_act = jax.nn.silu(node_pre).astype(BF16)
        node_sum = dot("snh,lh->snl", node_act, second_node) + params[5]
        node_update, node_normed, node_inverse = norm_forward(node_sum, params[6], params[7])
        node_state = node_state + node_update
        stashed.append(
            (
                node_low,
                table,
                edge_low,
                edge_pre,
                edge_act,
                edge_normed,
                edge_inverse,
                pooled,
                node_pre,
                node_act,
                node_normed,
                node_inverse,
            )
        )
        node_low = node_state.astype(BF16)
        edge_low = edge_next
    node_out = jnp.transpose(own_nodes(node_low), (1, 0, 2))

    node_grad = target
    edge_grad = None
    reduced = [None] * LAYERS
    minor_local = [None] * LAYERS
    carried = None
    for depth in reversed(range(LAYERS)):
        (
            node_low,
            table,
            edge_low,
            edge_pre,
            edge_act,
            edge_normed,
            edge_inverse,
            pooled,
            node_pre,
            node_act,
            node_normed,
            node_inverse,
        ) = stashed[depth]
        params = small_params[depth]
        first_edge, second_edge = edge_weights[depth]
        own_weight = first_edge[:latent]
        send_weight = first_edge[latent : 2 * latent]
        recv_weight = first_edge[2 * latent :]
        first_node, second_node = node_weights[depth]

        node_sum_low = norm_backward(node_grad, node_normed, node_inverse, params[6]).astype(BF16)
        node_act_grad = dot("snl,lh->snh", node_sum_low, second_node)
        node_pre_grad = (node_act_grad * silu_slope(node_pre)).astype(BF16)
        node_input_grad = dot("snh,lh->snl", node_pre_grad, first_node[:latent])
        pooled_grad = dot("snh,lh->snl", node_pre_grad, first_node[latent:]).astype(BF16)
        mine_pre = own_nodes(node_pre_grad)
        mine_sum = own_nodes(node_sum_low)
        mine_grad = own_nodes(node_grad)
        mine_normed = own_nodes(node_normed)
        first_node_grad = jnp.concatenate(
            [
                dot("rl,rh->lh", flat(own_nodes(node_low)), flat(mine_pre)),
                dot("rl,rh->lh", flat(own_nodes(pooled)), flat(mine_pre)),
            ],
            axis=0,
        )
        second_node_grad = dot("rl,rh->lh", flat(mine_sum), flat(own_nodes(node_act)))

        gathered = dot("en,snl->sel", at_receiver, pooled_grad)
        if carried is None:
            edge_grad = gathered
        else:
            edge_grad = edge_grad + gathered + dot("seh,lh->sel", *carried)
        edge_sum_low = norm_backward(edge_grad, edge_normed, edge_inverse, params[2]).astype(BF16)
        edge_act_grad = dot("sel,lh->seh", edge_sum_low, second_edge)
        edge_pre_grad = (edge_act_grad * silu_slope(edge_pre)).astype(BF16)
        at_nodes = dot("en,seh->snh", at_both, edge_pre_grad).astype(BF16)
        table_pre = at_nodes[:, :table_total]
        receiver_pre = at_nodes[:, table_total:]
        returned = to_neighbours_back(
            dot("snh,lh->snl", table_pre[:, node_total:], send_weight).astype(BF16), halo_width
        )
        partial = (
            dot("snh,lh->snl", table_pre[:, :node_total], send_weight)
            + dot("snh,lh->snl", receiver_pre, recv_weight)
            + dot("hn,shl->snl", at_halo, returned)
        )
        second_edge_grad = dot("rl,rh->lh", flat(edge_sum_low), flat(edge_act))
        if depth == 0:
            own_weight_grad = dot(
                "el,eh->lh", edge_low, jnp.sum(edge_pre_grad.astype(F32), axis=0).astype(BF16)
            )
        else:
            own_weight_grad = dot("rl,rh->lh", flat(edge_low), flat(edge_pre_grad))
        first_edge_grad = jnp.concatenate(
            [
                own_weight_grad,
                dot("rl,rh->lh", flat(table), flat(table_pre)),
                dot("rl,rh->lh", flat(node_low), flat(receiver_pre)),
            ],
            axis=0,
        )
        reduced[depth] = (
            *scatter_pair(first_edge_grad, second_edge_grad),
            *scatter_pair(first_node_grad, second_node_grad),
        )
        minor_local[depth] = jnp.stack(
            [
                jnp.sum(edge_pre_grad.astype(F32), axis=(0, 1)),
                jnp.sum(edge_sum_low.astype(F32), axis=(0, 1)),
                jnp.sum(edge_grad * edge_normed, axis=(0, 1)),
                jnp.sum(edge_grad, axis=(0, 1)),
                jnp.sum(mine_pre.astype(F32), axis=(0, 1)),
                jnp.sum(mine_sum.astype(F32), axis=(0, 1)),
                jnp.sum(mine_grad * mine_normed, axis=(0, 1)),
                jnp.sum(mine_grad, axis=(0, 1)),
            ]
        )
        if depth > 0:
            carried = (edge_pre_grad, own_weight)
            node_grad = node_grad + node_input_grad + sum_rows_spread(partial).astype(F32)
        else:
            node_grad = mine_grad + own_nodes(node_input_grad) + sum_rows(partial)
            edge_input_grad = jnp.sum(edge_grad, axis=0) + dot(
                "eh,lh->el", jnp.sum(edge_pre_grad.astype(F32), axis=0).astype(BF16), own_weight
            )
    grad_node = jnp.transpose(node_grad.astype(BF16), (1, 0, 2))

    weight_local = jnp.stack([jnp.sum(matrix * matrix, axis=(1, 2)) for matrix in masters], axis=1)
    weight_squares = sum_everywhere(weight_local)
    minor_total = sum_everywhere(jnp.stack(minor_local))
    grads = [jnp.stack([reduced[depth][place] for depth in range(LAYERS)]) for place in range(4)]
    firsts = (edge_first_m, edge_second_m, node_first_m, node_second_m)
    seconds = (edge_first_v, edge_second_v, node_first_v, node_second_v)
    moment_list = [
        adam_terms(masters[place], grads[place], firsts[place], seconds[place], WEIGHT_DECAY)
        for place in range(4)
    ]
    update_squares = sum_everywhere(
        jnp.stack([jnp.sum(entry[2] * entry[2], axis=(1, 2)) for entry in moment_list], axis=1)
    )
    weight_norm = jnp.sqrt(weight_squares)
    update_norm = jnp.sqrt(update_squares)
    new_weights = []
    for position in range(4):
        ratio = weight_norm[:, position] / update_norm[:, position]
        new_weights.append(
            masters[position] - learn_rate[0] * ratio[:, None, None] * moment_list[position][2]
        )
    small_first, small_second, small_update = adam_terms(
        small_params, minor_total, small_m, small_v, 0.0
    )
    small_wnorm = jnp.sqrt(jnp.sum(small_params * small_params, axis=2))
    small_unorm = jnp.sqrt(jnp.sum(small_update * small_update, axis=2))
    small_new = (
        small_params - learn_rate[0] * (small_wnorm / small_unorm)[:, :, None] * small_update
    )
    norms = jnp.stack(
        [
            jnp.concatenate([weight_norm, small_wnorm], axis=1),
            jnp.concatenate([update_norm, small_unorm], axis=1),
        ],
        axis=2,
    )
    return (
        node_out,
        grad_node,
        edge_input_grad.astype(BF16),
        *new_weights,
        *[entry[0] for entry in moment_list],
        *[entry[1] for entry in moment_list],
        *[weight.astype(BF16) for weight in new_weights],
        small_new,
        small_first,
        small_second,
        norms,
    )


def to_neighbours_back(rows, halo_width):
    count = lax.axis_size("node")
    onward = [(i, (i + 1) % count) for i in range(count)]
    back = [(target, source) for source, target in onward]
    from_previous = lax.ppermute(rows[:, halo_width:], "node", onward)
    from_next = lax.ppermute(rows[:, :halo_width], "node", back)
    return jnp.concatenate([from_previous, from_next], axis=1)


def solution(mesh):
    whole = P()
    rows = P(None, "node", "hid")
    columns = P(None, "hid", "node")
    matrices = (rows, columns, rows, columns)
    in_specs = (
        P("node", None, None),
        P("node", None),
        P(("node", "hid"), None, None),
        P(("node", "hid")),
        P(("node", "hid"), None),
        P(),
        P("node"),
        P("node"),
        P("node", None),
        *matrices,
        *matrices,
        *matrices,
        whole,
        whole,
        whole,
        whole,
    )
    out_specs = (
        P(("node", "hid"), None, None),
        P(("node", "hid"), None, None),
        P(("node", "hid"), None),
        *matrices,
        *matrices,
        *matrices,
        *matrices,
        whole,
        whole,
        whole,
        whole,
    )
    return jax.shard_map(
        per_device, mesh=mesh, in_specs=in_specs, out_specs=out_specs, check_vma=False
    )
```

time: 2180 us -> 848 us (0.39)
  other arithmetic: 1000 us -> 76.5 us
  local copies, waits for them, and re-layouts: 320 us -> 61.3 us
  blocking collectives: 196 us -> 0 us
  waiting for transfers between devices: 451 us -> 547 us
  matrix products: 145 us -> 96.1 us
    scatter-add x8 -> x0, other arithmetic: 922 us -> none  [the longest x2 336 us: hidden_pass(): jax.ops.segment_sum(send_back, send_slot, num_segments=node_total + 2 * h...]
    all_gather x7 -> x0, blocking collectives: 157 us -> none  [the longest x1 36.5 us: per_device(): lax.all_gather(edge_first.astype(jnp.bfloat16), 'node', axis=1, tiled=True)]
    dot_general x10 -> x0, local copies, waits for them, and re-layouts: 118 us -> none  [the longest x2 56.7 us: hidden_pass(): jnp.einsum('esh,lh->esl', edge_pre_grad, send_weight, preferred_element_t...]
    gather x13 -> x0, local copies, waits for them, and re-layouts: 104 us -> none  [the longest x2 33.3 us: hidden_pass(): node_low[recv_local]]
    ppermute x8 -> x39, waiting for transfers between devices: 0.47 us -> 84.6 us  [the longest x31 64.5 us: swap(): return lax.ppermute(values, axis, [(i, i ^ 1 << bit) for i in range(count)])]
    unnamed x20 -> x8, waiting for transfers between devices: 74.5 us -> 0.13 us
    reduce_scatter x6 -> x4, waiting for transfers between devices: 269 us -> 338 us  [scatter_pair(): lax.psum_scatter(packed.reshape(-1, width), ('node', 'hid'), scatter_dime...]
    dot_general x42 -> x54, matrix products: 145 us -> 96.1 us  [dot(): return jnp.einsum(spec, left, right, preferred_element_type=F32)]
  transfers between devices with their start and end apart: 23 -> 47, of which waited for: 11 -> 36; matrix products, arithmetic and copies ran while one was open for 35% -> 20% of each run, Pallas kernels for 0% -> 0%
where the time goes in v1:
time: 848 us; the launch traced here: 840 us
  waiting for transfers between devices  547 us (65%)
  matrix products  96.1 us (11%)
  other arithmetic  76.5 us (9%)
  local copies, waits for them, and re-layouts  61.3 us (7%)
  starting transfers between devices  41.5 us (5%)
  between operations  17.4 us (2%)
    reduce_scatter x4, waiting for transfers between devices, scatter_pair(): lax.psum_scatter(packed.reshape(-1, width), ('node', 'hid'), scatter_dime...  338 us
    all_gather x4, waiting for transfers between devices, gather_pair(): whole = lax.all_gather(packed, ('node', 'hid'), axis=0, tiled=True)  124 us
    dot_general x54, matrix products, dot(): return jnp.einsum(spec, left, right, preferred_element_type=F32)  96.1 us
    ppermute x31, waiting for transfers between devices, swap(): return lax.ppermute(values, axis, [(i, i ^ 1 << bit) for i in range(count)])  64.5 us
    unnamed x291, local copies, waits for them, and re-layouts  22 us
    ppermute x31, starting transfers between devices, swap(): return lax.ppermute(values, axis, [(i, i ^ 1 << bit) for i in range(count)])  20 us
  transfers between devices with their start and end apart: 47, of which 36 were waited for; matrix products, arithmetic and copies ran while one was open for 20% of the time, Pallas kernels for 0%

profile of v1, /device:TPU:0, one launch (start us, length us, event | category | flops | bytes accessed | tf_op | source)
XLA Modules:
  0.0 840.2 jit_solution(10270168468214572414)
XLA Ops:
  13.5 3.0 collective-permute-start
  16.5 3.1 collective-permute-start.1
  23.7 48.1 %all-gather.7.cloned.1.call-done = bf16[8192,128]{1,0:T(8,128)(2,1)} async-done(((bf16[256,128]{1,0:T(8,128)(2,1)}), bf16[8192,128]{1,0:T(8,128)(2,1)}) %all-gather.7.cloned.1.call-update) | async-done | bytes 2097168 | tf_op jit(solution)/shard_map/all_gather | solution.py:123
  77.3 3.4 multiply_convert_fusion.5
  93.2 6.6 collective-permute-done.3
  103.4 25.7 %all-gather.5.cloned.1.call-done = bf16[6144,128]{1,0:T(8,128)(2,1)} async-done(((bf16[192,128]{1,0:T(8,128)(2,1)}), bf16[6144,128]{1,0:T(8,128)(2,1)}) %all-gather.5.cloned.1.call-update) | async-done | bytes 1572880 | tf_op jit(solution)/shard_map/all_gather | solution.py:123
  137.5 50.2 %all-gather.11.cloned.1.call-done = bf16[8192,128]{1,0:T(8,128)(2,1)} async-done(((bf16[256,128]{1,0:T(8,128)(2,1)}), bf16[8192,128]{1,0:T(8,128)(2,1)}) %all-gather.11.cloned.1.call-update) | async-done | bytes 2097168 | tf_op jit(solution)/shard_map/all_gather | solution.py:123
  201.5 3.3 collective-permute-start.7
  205.5 6.9 collective-permute-done.6
  217.0 3.7 multiply_convert_fusion.4
  232.7 9.4 %collective-permute-done.9 = bf16[6,40,512]{2,1,0:T(8,128)(2,1)S(1)} collective-permute-done((bf16[6,40,512]{2,1,0:T(8,128)(2,1)S(1)}, bf16[6,40,512]{2,1,0:T(8,128)(2,1)S(1)}, u32[]{:S(2)}, u32[]{:S(2)}) %collective-permute-start.9) | collective-permute-done | bytes 245792 | tf_op jit(solution)/shard_map/ppermute | solution.py:46
  242.9 4.5 collective-permute-done.12
  271.6 7.7 fusion.1
  280.7 4.8 convert_reduce_fusion
  293.3 3.4 collective-permute-start.15
  297.4 6.8 collective-permute-done.14
  310.0 7.5 collective-permute-done.17
  321.1 4.5 collective-permute-done.18
  347.5 3.1 multiply_convert_fusion.6
  359.8 3.4 fusion.35
  371.6 3.6 convert_element_type.403
  385.0 4.3 fusion.29
  389.4 7.8 multiply_reduce_fusion
  399.7 3.7 convert_reduce_fusion.3
  406.1 3.1 convert_bitcast_fusion.1
  410.0 4.7 collective-permute-start.21
  442.5 7.0 collective-permute-done.23
  461.0 3.7 collective-permute-done.37
  465.9 3.7 collective-permute-done.38
  470.4 63.9 %reduce-scatter.9.cloned.1.call-done = bf16[192,128]{1,0:T(8,128)(2,1)} async-done(((bf16[6144,128]{1,0:T(8,128)(2,1)}), bf16[192,128]{1,0:T(8,128)(2,1)}) %reduce-scatter.9.cloned.1.call-update) | async-done | bytes 49168 | tf_op jit(solution)/shard_map/reduce_scatter | solution.py:144
  535.6 138.6 %reduce-scatter.7.cloned.1.call-done = bf16[256,128]{1,0:T(8,128)(2,1)} async-done(((bf16[8192,128]{1,0:T(8,128)(2,1)}), bf16[256,128]{1,0:T(8,128)(2,1)}) %reduce-scatter.7.cloned.1.call-update) | async-done | bytes 65552 | tf_op jit(solution)/shard_map/reduce_scatter | solution.py:144
  675.0 135.7 %reduce-scatter.5.cloned.1.call-done = bf16[256,128]{1,0:T(8,128)(2,1)} async-done(((bf16[8192,128]{1,0:T(8,128)(2,1)}), bf16[256,128]{1,0:T(8,128)(2,1)}) %reduce-scatter.5.cloned.1.call-update) | async-done | bytes 65552 | tf_op jit(solution)/shard_map/reduce_scatter | solution.py:144
  (595 shorter events, 233.7 us)
Async XLA Ops:
  7.2 64.6 %all-gather.7.cloned.1.call-start = ((), (), s32[]{:S(2)}) async-start(), calls=%async_computation.5 | async-start | bytes 2162688 | tf_op jit(solution)/shard_map/all_gather | solution.py:123
  9.8 119.3 %all-gather.5.cloned.1.call-start = ((), (), s32[]{:S(2)}) async-start(), calls=%async_computation.4 | async-start | bytes 1622016 | tf_op jit(solution)/shard_map/all_gather | solution.py:123
  12.3 175.4 %all-gather.11.cloned.1.call-start = ((), (), s32[]{:S(2)}) async-start(), calls=%async_computation.7 | async-start | bytes 2162688 | tf_op jit(solution)/shard_map/all_gather | solution.py:123
  13.5 61.5 %collective-permute-start = (bf16[6,40,512]{2,1,0:T(8,128)(2,1)S(1)}, bf16[6,40,512]{2,1,0:T(8,128)(2,1)S(1)}, u32[]{:S(2)}, u32[]{:S(2)}) collective-permute-start(bf16[6,40,512]{2,1,0:T(8,128)(2,1)S(1)} %get-tuple-element.192), channel_id=1, source_target_pairs={{0,4},{4,8},{8,12},{12,16},{16,20},{20,24},{24,28},{28,0},{1,5},{5... | collective-permute-start | bytes 737288 | tf_op jit(solution)/shard_map/ppermute | solution.py:108
  16.5 58.5 %collective-permute-start.1 = (bf16[6,40,512]{2,1,0:T(8,128)(2,1)S(1)}, bf16[6,40,512]{2,1,0:T(8,128)(2,1)}, u32[]{:S(2)}, u32[]{:S(2)}) collective-permute-start(bf16[6,40,512]{2,1,0:T(8,128)(2,1)S(1)} %get-tuple-element.193), channel_id=1, source_target_pairs={{4,0},{8,4},{12,8},{16,12},{20,16},{24,20},{28,24},{0,28},{5,1},{9... | collective-permute-start | bytes 737288 | tf_op jit(solution)/shard_map/ppermute | solution.py:109
  20.3 229.0 %all-gather.9.cloned.1.call-start = ((), (), s32[]{:S(2)}) async-start(), calls=%async_computation.6 | async-start | bytes 1622016 | tf_op jit(solution)/shard_map/all_gather | solution.py:123
  91.7 8.1 collective-permute-start.3
  100.9 30.7 %collective-permute-start.4 = (bf16[6,40,512]{2,1,0:T(8,128)(2,1)S(1)}, bf16[6,40,512]{2,1,0:T(8,128)(2,1)}, u32[]{:S(2)}, u32[]{:S(2)}) collective-permute-start(bf16[6,40,512]{2,1,0:T(8,128)(2,1)S(1)} %fusion.83), channel_id=1, source_target_pairs={{0,2},{1,3},{2,0},{3,1},{4,6},{5,7},{6,4},{7,5},{8,10},{9,11},{10,... | collective-permute-start | bytes 737288 | tf_op jit(solution)/shard_map/ppermute | solution.py:46
  103.1 355.9 %reduce-scatter.11.cloned.1.call-start = ((), (), s32[]{:S(2)}) async-start(), calls=%async_computation.11 | async-start | bytes 1622016 | tf_op jit(solution)/shard_map/reduce_scatter | solution.py:144
  133.6 56.3 %collective-permute-start.5 = (bf16[2,6,40,512]{3,2,1,0:T(8,128)(2,1)}, bf16[2,6,40,512]{3,2,1,0:T(8,128)(2,1)}, u32[]{:S(2)}, u32[]{:S(2)}) collective-permute-start(bf16[2,6,40,512]{3,2,1,0:T(8,128)(2,1)} %pad_maximum_fusion.11), channel_id=1, source_target_pairs={{0,1},{1,0},{2,3},{3,2},{4,5},{5,4},{6,7},{7,6},{8,9},{9,8},{10,11... | collective-permute-start | bytes 1474568 | tf_op jit(solution)/shard_map/ppermute | solution.py:46
  200.1 12.3 %collective-permute-start.6 = (bf16[6,40,512]{2,1,0:T(8,128)(2,1)S(1)}, bf16[6,40,512]{2,1,0:T(8,128)(2,1)S(1)}, u32[]{:S(2)}, u32[]{:S(2)}) collective-permute-start(bf16[6,40,512]{2,1,0:T(8,128)(2,1)S(1)} %get-tuple-element.188), channel_id=1, source_target_pairs={{0,4},{4,8},{8,12},{12,16},{16,20},{20,24},{24,28},{28,0},{1,5},{5... | collective-permute-start | bytes 737288 | tf_op jit(solution)/shard_map/ppermute | solution.py:108
  201.5 13.1 %collective-permute-start.7 = (bf16[6,40,512]{2,1,0:T(8,128)(2,1)S(1)}, bf16[6,40,512]{2,1,0:T(8,128)(2,1)S(1)}, u32[]{:S(2)}, u32[]{:S(2)}) collective-permute-start(bf16[6,40,512]{2,1,0:T(8,128)(2,1)S(1)} %get-tuple-element.189), channel_id=1, source_target_pairs={{4,0},{8,4},{12,8},{16,12},{20,16},{24,20},{28,24},{0,28},{5,1},{9... | collective-permute-start | bytes 737288 | tf_op jit(solution)/shard_map/ppermute | solution.py:109
  230.4 11.7 %collective-permute-start.9 = (bf16[6,40,512]{2,1,0:T(8,128)(2,1)S(1)}, bf16[6,40,512]{2,1,0:T(8,128)(2,1)S(1)}, u32[]{:S(2)}, u32[]{:S(2)}) collective-permute-start(bf16[6,40,512]{2,1,0:T(8,128)(2,1)S(1)} %fusion.90), channel_id=1, source_target_pairs={{0,2},{1,3},{2,0},{3,1},{4,6},{5,7},{6,4},{7,5},{8,10},{9,11},{10,... | collective-permute-start | bytes 737288 | tf_op jit(solution)/shard_map/ppermute | solution.py:46
  231.2 16.2 %collective-permute-start.12 = (bf16[6,40,512]{2,1,0:T(8,128)(2,1)S(1)}, bf16[6,40,512]{2,1,0:T(8,128)(2,1)S(1)}, u32[]{:S(2)}, u32[]{:S(2)}) collective-permute-start(bf16[6,40,512]{2,1,0:T(8,128)(2,1)S(1)} %multiply_bitcast_fusion), channel_id=1, source_target_pairs={{0,2},{1,3},{2,0},{3,1},{4,6},{5,7},{6,4},{7,5},{8,10},{9,11},{10,... | collective-permute-start | bytes 737288 | tf_op jit(solution)/shard_map/ppermute | solution.py:46
  242.2 9.7 %collective-permute-start.10 = (bf16[6,40,512]{2,1,0:T(8,128)(2,1)S(1)}, bf16[6,40,512]{2,1,0:T(8,128)(2,1)S(1)}, u32[]{:S(2)}, u32[]{:S(2)}) collective-permute-start(bf16[6,40,512]{2,1,0:T(8,128)(2,1)S(1)} %fusion.82), channel_id=1, source_target_pairs={{0,2},{1,3},{2,0},{3,1},{4,6},{5,7},{6,4},{7,5},{8,10},{9,11},{10,... | collective-permute-start | bytes 737288 | tf_op jit(solution)/shard_map/ppermute | solution.py:46
  249.0 6.0 collective-permute-start.13
  291.8 12.5 %collective-permute-start.14 = (bf16[6,40,512]{2,1,0:T(8,128)(2,1)S(1)}, bf16[6,40,512]{2,1,0:T(8,128)(2,1)S(1)}, u32[]{:S(2)}, u32[]{:S(2)}) collective-permute-start(bf16[6,40,512]{2,1,0:T(8,128)(2,1)S(1)} %get-tuple-element.184), channel_id=1, source_target_pairs={{0,4},{4,8},{8,12},{12,16},{16,20},{20,24},{24,28},{28,0},{1,5},{5... | collective-permute-start | bytes 737288 | tf_op jit(solution)/shard_map/ppermute | solution.py:437
  293.3 13.3 %collective-permute-start.15 = (bf16[6,40,512]{2,1,0:T(8,128)(2,1)S(1)}, bf16[6,40,512]{2,1,0:T(8,128)(2,1)S(1)}, u32[]{:S(2)}, u32[]{:S(2)}) collective-permute-start(bf16[6,40,512]{2,1,0:T(8,128)(2,1)S(1)} %get-tuple-element.185), channel_id=1, source_target_pairs={{4,0},{8,4},{12,8},{16,12},{20,16},{24,20},{28,24},{0,28},{5,1},{9... | collective-permute-start | bytes 737288 | tf_op jit(solution)/shard_map/ppermute | solution.py:438
  309.4 8.1 collective-permute-start.17
  318.2 7.4 collective-permute-start.18
  327.4 10.1 %collective-permute-start.19 = (bf16[2,6,40,512]{3,2,1,0:T(8,128)(2,1)}, bf16[2,6,40,512]{3,2,1,0:T(8,128)(2,1)}, u32[]{:S(2)}, u32[]{:S(2)}) collective-permute-start(bf16[2,6,40,512]{3,2,1,0:T(8,128)(2,1)} %pad_maximum_fusion.14), channel_id=1, source_target_pairs={{0,1},{1,0},{2,3},{3,2},{4,5},{5,4},{6,7},{7,6},{8,9},{9,8},{10,11... | collective-permute-start | bytes 1474568 | tf_op jit(solution)/shard_map/ppermute | solution.py:46
  335.1 199.2 %reduce-scatter.9.cloned.1.call-start = ((), (), s32[]{:S(2)}) async-start(), calls=%async_computation.10 | async-start | bytes 1622016 | tf_op jit(solution)/shard_map/reduce_scatter | solution.py:144
  359.5 314.6 %reduce-scatter.7.cloned.1.call-start = ((), (), s32[]{:S(2)}) async-start(), calls=%async_computation.9 | async-start | bytes 2162688 | tf_op jit(solution)/shard_map/reduce_scatter | solution.py:144
  384.2 426.5 %reduce-scatter.5.cloned.1.call-start = ((), (), s32[]{:S(2)}) async-start(), calls=%async_computation.8 | async-start | bytes 2162688 | tf_op jit(solution)/shard_map/reduce_scatter | solution.py:144
  409.7 12.4 %collective-permute-start.20 = (bf16[6,40,512]{2,1,0:T(8,128)(2,1)S(1)}, bf16[6,40,512]{2,1,0:T(8,128)(2,1)S(1)}, u32[]{:S(2)}, u32[]{:S(2)}) collective-permute-start(bf16[6,40,512]{2,1,0:T(8,128)(2,1)S(1)} %get-tuple-element.180), channel_id=1, source_target_pairs={{0,4},{4,8},{8,12},{12,16},{16,20},{20,24},{24,28},{28,0},{1,5},{5... | collective-permute-start | bytes 737288 | tf_op jit(solution)/shard_map/ppermute | solution.py:437
  410.0 14.0 %collective-permute-start.21 = (bf16[6,40,512]{2,1,0:T(8,128)(2,1)S(1)}, bf16[6,40,512]{2,1,0:T(8,128)(2,1)S(1)}, u32[]{:S(2)}, u32[]{:S(2)}) collective-permute-start(bf16[6,40,512]{2,1,0:T(8,128)(2,1)S(1)} %get-tuple-element.181), channel_id=1, source_target_pairs={{4,0},{8,4},{12,8},{16,12},{20,16},{24,20},{28,24},{0,28},{5,1},{9... | collective-permute-start | bytes 737288 | tf_op jit(solution)/shard_map/ppermute | solution.py:438
  426.7 12.7 %collective-permute-start.22 = (bf16[2,6,40,512]{3,2,1,0:T(8,128)(2,1)}, bf16[2,6,40,512]{3,2,1,0:T(8,128)(2,1)}, u32[]{:S(2)}, u32[]{:S(2)}) collective-permute-start(bf16[2,6,40,512]{3,2,1,0:T(8,128)(2,1)} %fusion.69), channel_id=1, source_target_pairs={{0,1},{1,0},{2,3},{3,2},{4,5},{5,4},{6,7},{7,6},{8,9},{9,8},{10,11... | collective-permute-start | bytes 1474568 | tf_op jit(solution)/shard_map/ppermute | solution.py:46
  441.0 8.4 %collective-permute-start.23 = (bf16[6,40,512]{2,1,0:T(8,128)(2,1)S(1)}, bf16[6,40,512]{2,1,0:T(8,128)(2,1)S(1)}, u32[]{:S(2)}, u32[]{:S(2)}) collective-permute-start(bf16[6,40,512]{2,1,0:T(8,128)(2,1)S(1)} %fusion.92), channel_id=1, source_target_pairs={{0,2},{1,3},{2,0},{3,1},{4,6},{5,7},{6,4},{7,5},{8,10},{9,11},{10,... | collective-permute-start | bytes 737288 | tf_op jit(solution)/shard_map/ppermute | solution.py:46
  456.7 4.0 collective-permute-start.36
  464.6 4.9 collective-permute-start.38
  824.2 4.5 collective-permute-start.28
  824.5 4.5 collective-permute-start.33
  (160 other events, 6246.5 us)
Sparse Core Ops, SparseCore 0:
  11.4 60.3 all-gather.6
  75.3 53.7 all-gather.4
  132.6 55.1 all-gather.10
  191.1 58.1 all-gather.8
  335.2 97.1 reduce-scatter.10
  437.4 96.8 reduce-scatter.8
  536.5 137.5 reduce-scatter.6
  676.4 134.2 reduce-scatter.4
